TPU v7x, 32 devices: a whole 2x2x4 slice. The times are simulated.
32 devices in a mesh: rows: 8 (over y, x, core), cols: 4 (over z).
Axes of the slice: x: 2, y: 2, z: 4, core: 2. Of those that a mesh axis runs over, the one named last changes fastest.
Arguments:
- block_inputs: bfloat16 [64, 128, 384], P('rows', 'cols'), may hold values from -12 to 12
- upstream_adjoint: bfloat16 [64, 128, 384], P('rows', 'cols'), may hold values from -12 to 12
- norm_factor: float32 [384], replicated, may hold values from 0.1 to 1.9
- triple_projection: bfloat16 [384, 1152], replicated, may hold values from -0.3125 to 0.3125
- spatial_filter_taps: bfloat16 [3, 3, 1152], replicated, may hold values from -2 to 2
- sharpness_factors: float32 [8], replicated, may hold values from 4 to 24
- final_projection: bfloat16 [384, 384], replicated, may hold values from -0.3125 to 0.3125
Outputs:
- inputs_adjoint: bfloat16 [64, 128, 384], P('rows', 'cols')
- norm_factor_adjoint: float32 [384], replicated
- spatial_filter_adjoint: float32 [3, 3, 1152], replicated
- sharpness_adjoint: float32 [8], replicated
All inputs are finite; a program needn't handle non-finite values.
Results may differ from a plain program's by a relative error of at most 0.0048.
Values may be sent and summed in bfloat16 or wider, within the bound.
A program may use at most 64 MiB of HBM per device.

v0:
```python
import jax
import jax.numpy as jnp
from jax import lax
from jax.sharding import PartitionSpec as P

norm_eps = 1e-05
unit_eps = 1e-06


def with_halo(x, sides, width):
    for axis, dim in sides:
        peers, length = (lax.axis_size(axis), x.shape[dim])
        up = [(i, (i + 1) % peers) for i in range(peers - 1)]
        down = [(j, i) for i, j in up]
        last = lax.slice_in_dim(x, length - width, length, axis=dim)
        leading = lax.slice_in_dim(x, 0, width, axis=dim)
        before = lax.ppermute(last, axis, up)
        after = lax.ppermute(leading, axis, down)
        x = jnp.concatenate([before, x, after], axis=dim)
    return x


def norm_project(tile_in, norm_factor, triple_projection):
    feat_f = tile_in.astype(jnp.float32)
    centred = feat_f - jnp.mean(feat_f, axis=-1, keepdims=True)
    inv_std = lax.rsqrt(jnp.mean(centred * centred, axis=-1, keepdims=True) + norm_eps)
    standard = centred * inv_std
    normed = (standard * norm_factor).astype(jnp.bfloat16)
    channels = tile_in.shape[2]
    projected = jnp.dot(
        normed.reshape(-1, channels), triple_projection, preferred_element_type=jnp.float32
    )
    qkv_tile = projected.astype(jnp.bfloat16).reshape(
        tile_in.shape[0], tile_in.shape[1], 3 * channels
    )
    return (standard, inv_std, qkv_tile)


def conv_forward(padded, taps, block_rows, block_cols):
    total = jnp.zeros((block_rows, block_cols, padded.shape[2]), jnp.float32)
    for tap_row in range(3):
        for tap_col in range(3):
            total = total + taps[tap_row, tap_col] * padded[
                tap_row : tap_row + block_rows, tap_col : tap_col + block_cols
            ].astype(jnp.float32)
    return total


def conv_backward(padded, taps, block_rows, block_cols):
    total = jnp.zeros((block_rows, block_cols, padded.shape[2]), jnp.float32)
    for tap_row in range(3):
        for tap_col in range(3):
            total = total + taps[tap_row, tap_col] * padded[
                2 - tap_row : 2 - tap_row + block_rows, 2 - tap_col : 2 - tap_col + block_cols
            ].astype(jnp.float32)
    return total


def kernel_terms(padded, grad_mixed, block_rows, block_cols):
    grad_f = grad_mixed.astype(jnp.float32)
    kernel_rows = []
    for tap_row in range(3):
        kernel_cols = []
        for tap_col in range(3):
            window = padded[tap_row : tap_row + block_rows, tap_col : tap_col + block_cols].astype(
                jnp.float32
            )
            kernel_cols.append(jnp.sum(window * grad_f, axis=(0, 1)))
        kernel_rows.append(jnp.stack(kernel_cols))
    return jnp.stack(kernel_rows)


def local(
    block_inputs,
    upstream_adjoint,
    norm_factor,
    triple_projection,
    spatial_filter_taps,
    sharpness_factors,
    final_projection,
):
    block_rows, block_cols, channels = block_inputs.shape
    group_total = sharpness_factors.shape[0]
    head_size = channels // group_total
    positions = block_rows * block_cols
    pixel_amount = positions * lax.axis_size("rows") * lax.axis_size("cols")
    highest = lax.Precision.HIGHEST
    taps = spatial_filter_taps.astype(jnp.float32)
    margin = 0
    standard, inv_std, qkv_local = norm_project(block_inputs, norm_factor, triple_projection)
    qkv_padded = with_halo(qkv_local, (("rows", 0), ("cols", 1)), 1)
    wide_rows = block_rows + 2 * margin
    wide_cols = block_cols + 2 * margin
    convolved_wide = conv_forward(qkv_padded, taps, wide_rows, wide_cols).reshape(
        wide_rows, wide_cols, 3, group_total, head_size
    )
    grad_out_wide = jnp.dot(
        upstream_adjoint.reshape(wide_rows * wide_cols, channels),
        final_projection.T,
        preferred_element_type=jnp.float32,
    ).reshape(wide_rows, wide_cols, group_total, head_size)
    convolved = convolved_wide.reshape(positions, 3, group_total, head_size)
    queries = convolved[:, 0]
    keys_part = convolved[:, 1]
    values = convolved[:, 2]
    grad_out = grad_out_wide.reshape(positions, group_total, head_size)
    local_attn = jnp.einsum("phc,phd->hcd", grad_out, values, precision=highest)
    query_squares = jnp.sum(queries * queries, axis=0)
    keys_squares = jnp.sum(keys_part * keys_part, axis=0)
    query_total, keys_total = lax.psum((query_squares, keys_squares), ("rows", "cols"))
    query_scale = lax.rsqrt(query_total + unit_eps)
    keys_scale = lax.rsqrt(keys_total + unit_eps)
    similarity_table = lax.psum(
        jnp.einsum(
            "phc,phd->hcd", queries * query_scale, keys_part * keys_scale, precision=highest
        ),
        ("rows", "cols"),
    )
    grad_attention = lax.psum(local_attn, ("rows", "cols"))
    wide_flat = convolved_wide.reshape(wide_rows * wide_cols, 3, group_total, head_size)
    query_unit = wide_flat[:, 0] * query_scale
    keys_unit = wide_flat[:, 1] * keys_scale
    grad_out_flat = grad_out_wide.reshape(wide_rows * wide_cols, group_total, head_size)
    group_sharpness = sharpness_factors[:, None, None]
    exponent_probs = jnp.exp(group_sharpness * similarity_table)
    attention = exponent_probs / jnp.sum(exponent_probs, axis=-1, keepdims=True)
    grad_values = jnp.einsum("phc,hcd->phd", grad_out_flat, attention, precision=highest)
    logits_adjoint = attention * (
        grad_attention - jnp.sum(attention * grad_attention, axis=-1, keepdims=True)
    )
    sharpness_adjoint = jnp.sum(logits_adjoint * similarity_table, axis=(1, 2)) / pixel_amount
    similarity_adjoint = group_sharpness * logits_adjoint
    grad_qunit = jnp.einsum("phd,hcd->phc", keys_unit, similarity_adjoint, precision=highest)
    grad_kunit = jnp.einsum("phc,hcd->phd", query_unit, similarity_adjoint, precision=highest)
    query_local = jnp.sum(
        (query_unit * grad_qunit).reshape(wide_rows, wide_cols, group_total, head_size), axis=(0, 1)
    )
    keys_local = jnp.sum(
        (keys_unit * grad_kunit).reshape(wide_rows, wide_cols, group_total, head_size), axis=(0, 1)
    )
    query_dots, keys_dots = lax.psum((query_local, keys_local), ("rows", "cols"))
    grad_query = query_scale * (grad_qunit - query_unit * query_dots)
    grad_keys = keys_scale * (grad_kunit - keys_unit * keys_dots)
    grad_mixed_wide = (
        jnp.stack([grad_query, grad_keys, grad_values], axis=1)
        .astype(jnp.bfloat16)
        .reshape(wide_rows, wide_cols, 3 * channels)
    )
    grad_padded = with_halo(grad_mixed_wide, (("rows", 0), ("cols", 1)), 1)
    kernel_local = kernel_terms(qkv_padded, grad_mixed_wide, block_rows, block_cols)
    grad_qkv = (
        conv_backward(grad_padded, taps, block_rows, block_cols)
        .astype(jnp.bfloat16)
        .reshape(positions, 3 * channels)
    )
    standardized_adjoint = jnp.dot(
        grad_qkv, triple_projection.T, preferred_element_type=jnp.float32
    )
    standard_flat = standard.reshape(positions, channels)
    gain_local = jnp.sum(standardized_adjoint * standard_flat, axis=0)
    kernel_sum, gain_sum = lax.psum((kernel_local, gain_local), ("rows", "cols"))
    scaled = standardized_adjoint * norm_factor
    grad_input = inv_std.reshape(positions, 1) * (
        scaled
        - jnp.mean(scaled, axis=-1, keepdims=True)
        - standard_flat * jnp.mean(scaled * standard_flat, axis=-1, keepdims=True)
    )
    inputs_adjoint = (
        (upstream_adjoint.reshape(positions, channels).astype(jnp.float32) + grad_input)
        .astype(jnp.bfloat16)
        .reshape(block_rows, block_cols, channels)
    )
    return (inputs_adjoint, gain_sum / pixel_amount, kernel_sum / pixel_amount, sharpness_adjoint)


def solution(mesh):
    return jax.shard_map(
        local,
        mesh=mesh,
        in_specs=(P("rows", "cols", None), P("rows", "cols", None), P(), P(), P(), P(), P()),
        out_specs=(P("rows", "cols", None), P(), P(), P()),
        check_vma=False,
    )
```

profile of v0, /device:TPU:0, one launch (start us, length us, event | category | flops | bytes accessed | tf_op | source)
XLA Modules:
  0.0 364.5 jit_solution(5115874373106271304)
XLA Ops:
  9.5 1.9 multiply_convert_fusion
  11.9 2.4 collective-permute-start
  16.6 2.9 collective-permute-done.1
  19.6 3.5 collective-permute-start.2
  24.8 4.2 %collective-permute-done.3 = bf16[10,1,1152]{2,1,0:T(2,128)(2,1)S(1)} collective-permute-done((bf16[10,1,1152]{2,1,0:T(2,128)(2,1)S(1)}, bf16[10,1,1152]{2,1,0:T(2,128)(2,1)S(1)}, u32[]{:S(2)}, u32[]{:S(2)}) %collective-permute-start.3) | collective-permute-done | bytes 23072 | tf_op jit(solution)/shard_map/ppermute | solution.py:18
  29.5 1.9 fusion.7
  31.4 3.5 reshape_reshape.2
  34.9 3.7 %fusion.51 = (f32[256,1,8,48]{3,2,1,0:T(8,128)}, f32[256,1,8,48]{3,2,1,0:T(8,128)}, f32[256,1,8,48]{3,2,1,0:T(8,128)}) fusion(f32[256,3,8,48]{3,2,1,0:T(8,128)} %reshape_reshape.2), kind=kLoop, calls=%fused_computation.139 | loop fusion | bytes 2359296 | tf_op jit(solution)/shard_map/slice | solution.py:105
  38.6 2.3 copy.33
  42.0 2.3 copy.32
  45.4 2.3 copy.34
  47.8 41.9 %all-reduce.2 = (f32[8,48]{1,0:T(8,128)S(1)}, f32[8,48]{1,0:T(8,128)S(1)}) all-reduce(f32[8,48]{1,0:T(8,128)S(1)} %fusion.37, f32[8,48]{1,0:T(8,128)S(1)} %fusion.38), channel_id=1, replica_groups=mesh['rows'=8,'cols'=4] {'rows','cols'}, use_global_device_ids=true, to_apply=%region_5.0 | all-reduce | flops 768 | bytes 6144 | tf_op jit(solution)/shard_map/psum | solution.py:110
  89.6 2.5 fusion.39
  93.9 128.2 %all-reduce.6.cloned.1.call-done = (f32[8,48,48]{2,1,0:T(8,128)}, f32[8,48,48]{2,1,0:T(8,128)}) async-done(((f32[8,48,48]{2,1,0:T(8,128)}, f32[8,48,48]{2,1,0:T(8,128)}), (f32[8,48,48]{2,1,0:T(8,128)}, f32[8,48,48]{2,1,0:T(8,128)})) %all-reduce.6.cloned.1.call-update) | async-done | bytes 147472 | tf_op jit(solution)/shard_map/psum | solution.py:113
  224.7 3.3 multiply_reduce_fusion.2
  228.0 2.9 multiply_reduce_fusion.1
  232.2 39.7 %all-reduce.1 = (f32[8,48]{1,0:T(8,128)}, f32[8,48]{1,0:T(8,128)}) all-reduce(f32[8,48]{1,0:T(8,128)} %get-tuple-element.52, f32[8,48]{1,0:T(8,128)} %get-tuple-element.54), channel_id=1, replica_groups=mesh['rows'=8,'cols'=4] {'rows','cols'}, use_global_device_ids=true, to_apply=%region_13.0 | all-reduce | flops 768 | bytes 6144 | tf_op jit(solution)/shard_map/psum | solution.py:141
  275.0 2.6 copy.27
  277.6 2.2 bitcast_convert_fusion
  280.8 3.1 convert_element_type.118
  283.9 2.7 fusion.14
  302.0 4.5 %collective-permute-start.7 = (bf16[10,1,1152]{2,1,0:T(2,128)(2,1)S(1)}, bf16[10,1,1152]{2,1,0:T(2,128)(2,1)S(1)}, u32[]{:S(2)}, u32[]{:S(2)}) collective-permute-start(bf16[10,1,1152]{2,1,0:T(2,128)(2,1)S(1)} %get-tuple-element.41), channel_id=1, source_target_pairs={{0,1},{1,2},{2,3},{4,5},{5,6},{6,7},{8,9},{9,10},{10,11},{12,13},{... | collective-permute-start | bytes 69128 | tf_op jit(solution)/shard_map/ppermute | solution.py:17
  308.3 2.8 fusion.13
  311.8 43.8 %all-reduce = (f32[384]{0:T(512)S(1)}, f32[3,3,1152]{2,1,0:T(4,128)S(1)}) all-reduce(f32[384]{0:T(512)S(1)} %get-tuple-element.12, f32[3,3,1152]{2,1,0:T(4,128)S(1)} %pad_maximum_fusion.7), channel_id=1, replica_groups=mesh['rows'=8,'cols'=4] {'rows','cols'}, use_global_device_ids=true, to_apply=%region_17.0 | all-reduce | flops 10752 | bytes 86016 | tf_op jit(solution)/shard_map/psum | solution.py:161
  (145 shorter events, 38.8 us)
Async XLA Ops:
  7.2 215.0 %all-reduce.6.cloned.1.call-start = ((), (), s32[]{:S(2)}) async-start(), calls=%async_computation | async-start | bytes 786432 | tf_op jit(solution)/shard_map/psum | solution.py:113
  11.9 4.7 %collective-permute-start = (bf16[1,32,1152]{2,1,0:T(8,128)(2,1)S(1)}, bf16[1,32,1152]{2,1,0:T(8,128)(2,1)S(1)}, u32[]{:S(2)}, u32[]{:S(2)}) collective-permute-start(bf16[1,32,1152]{2,1,0:T(8,128)(2,1)S(1)} %get-tuple-element.48), channel_id=1, source_target_pairs={{0,4},{4,8},{8,12},{12,16},{16,20},{20,24},{24,28},{1,5},{5,9},{9,... | collective-permute-start | bytes 221192 | tf_op jit(solution)/shard_map/ppermute | solution.py:17
  14.2 5.3 %collective-permute-start.1 = (bf16[1,32,1152]{2,1,0:T(8,128)(2,1)S(1)}, bf16[1,32,1152]{2,1,0:T(8,128)(2,1)S(1)}, u32[]{:S(2)}, u32[]{:S(2)}) collective-permute-start(bf16[1,32,1152]{2,1,0:T(8,128)(2,1)S(1)} %get-tuple-element.49), channel_id=1, source_target_pairs={{4,0},{8,4},{12,8},{16,12},{20,16},{24,20},{28,24},{5,1},{9,5},{13... | collective-permute-start | bytes 221192 | tf_op jit(solution)/shard_map/ppermute | solution.py:18
  16.6 12.8 %copy-start.15 = (bf16[1,32,1152]{2,1,0:T(8,128)(2,1)}, bf16[1,32,1152]{2,1,0:T(8,128)(2,1)S(1)}, u32[]{:S(2)}) copy-start(bf16[1,32,1152]{2,1,0:T(8,128)(2,1)S(1)} %collective-permute-done) | copy-start | bytes 221188
  19.5 9.9 %copy-start.16 = (bf16[1,32,1152]{2,1,0:T(8,128)(2,1)}, bf16[1,32,1152]{2,1,0:T(8,128)(2,1)S(1)}, u32[]{:S(2)}) copy-start(bf16[1,32,1152]{2,1,0:T(8,128)(2,1)S(1)} %collective-permute-done.1) | copy-start | bytes 221188
  19.6 5.2 %collective-permute-start.2 = (bf16[10,1,1152]{2,1,0:T(2,128)(2,1)S(1)}, bf16[10,1,1152]{2,1,0:T(2,128)(2,1)S(1)}, u32[]{:S(2)}, u32[]{:S(2)}) collective-permute-start(bf16[10,1,1152]{2,1,0:T(2,128)(2,1)S(1)} %get-tuple-element.44), channel_id=1, source_target_pairs={{0,1},{1,2},{2,3},{4,5},{5,6},{6,7},{8,9},{9,10},{10,11},{12,13},{... | collective-permute-start | bytes 69128 | tf_op jit(solution)/shard_map/ppermute | solution.py:17
  23.1 6.0 %collective-permute-start.3 = (bf16[10,1,1152]{2,1,0:T(2,128)(2,1)S(1)}, bf16[10,1,1152]{2,1,0:T(2,128)(2,1)S(1)}, u32[]{:S(2)}, u32[]{:S(2)}) collective-permute-start(bf16[10,1,1152]{2,1,0:T(2,128)(2,1)S(1)} %get-tuple-element.45), channel_id=1, source_target_pairs={{1,0},{2,1},{3,2},{5,4},{6,5},{7,6},{9,8},{10,9},{11,10},{13,12},{... | collective-permute-start | bytes 69128 | tf_op jit(solution)/shard_map/ppermute | solution.py:18
  89.6 132.6 %copy-start.37 = (f32[8]{0:T(128)S(1)}, f32[8]{0:T(128)}, u32[]{:S(2)}) copy-start(f32[8]{0:T(128)} %param.12) | copy-start | bytes 100
  291.3 6.3 %copy-start.11 = (f32[8,48,48]{2,1,0:T(8,128)S(1)}, f32[8,48,48]{2,1,0:T(8,128)}, u32[]{:S(2)}) copy-start(f32[8,48,48]{2,1,0:T(8,128)} %get-tuple-element.36) | copy-start | bytes 221188
  291.4 7.1 %copy-start.4 = (bf16[8,32,1152]{2,1,0:T(8,128)(2,1)S(1)}, bf16[8,32,1152]{2,1,0:T(8,128)(2,1)}, u32[]{:S(2)}) copy-start(bf16[8,32,1152]{2,1,0:T(8,128)(2,1)} %convert_element_type.118) | copy-start | bytes 1769476
  293.1 5.4 %collective-permute-start.4 = (bf16[1,32,1152]{2,1,0:T(8,128)(2,1)S(1)}, bf16[1,32,1152]{2,1,0:T(8,128)(2,1)S(1)}, u32[]{:S(2)}, u32[]{:S(2)}) collective-permute-start(bf16[1,32,1152]{2,1,0:T(8,128)(2,1)S(1)} %copy.26), channel_id=1, source_target_pairs={{0,4},{4,8},{8,12},{12,16},{16,20},{20,24},{24,28},{1,5},{5,9},{9,... | collective-permute-start | bytes 221192 | tf_op jit(solution)/shard_map/ppermute | solution.py:17
  294.6 13.7 %copy-start.22 = (f32[1152]{0:T(1024)S(1)}, f32[1152]{0:T(1024)}, u32[]{:S(2)}) copy-start(f32[1152]{0:T(1024)} %copy-done.21) | copy-start | bytes 13828
  294.6 13.7 %copy-start.24 = (f32[1152]{0:T(1024)S(1)}, f32[1152]{0:T(1024)}, u32[]{:S(2)}) copy-start(f32[1152]{0:T(1024)} %copy-done.23) | copy-start | bytes 13828
  294.6 13.7 %copy-start.26 = (f32[1152]{0:T(1024)S(1)}, f32[1152]{0:T(1024)}, u32[]{:S(2)}) copy-start(f32[1152]{0:T(1024)} %copy-done.25) | copy-start | bytes 13828
  294.6 13.7 %copy-start.28 = (f32[1152]{0:T(1024)S(1)}, f32[1152]{0:T(1024)}, u32[]{:S(2)}) copy-start(f32[1152]{0:T(1024)} %copy-done.27) | copy-start | bytes 13828
  294.6 13.6 %copy-start.30 = (f32[1152]{0:T(1024)S(1)}, f32[1152]{0:T(1024)}, u32[]{:S(2)}) copy-start(f32[1152]{0:T(1024)} %copy-done.29) | copy-start | bytes 13828
  294.6 13.6 %copy-start.32 = (f32[1152]{0:T(1024)S(1)}, f32[1152]{0:T(1024)}, u32[]{:S(2)}) copy-start(f32[1152]{0:T(1024)} %copy-done.31) | copy-start | bytes 13828
  294.6 5.8 %collective-permute-start.5 = (bf16[1,32,1152]{2,1,0:T(8,128)(2,1)S(1)}, bf16[1,32,1152]{2,1,0:T(8,128)(2,1)S(1)}, u32[]{:S(2)}, u32[]{:S(2)}) collective-permute-start(bf16[1,32,1152]{2,1,0:T(8,128)(2,1)S(1)} %copy.28), channel_id=1, source_target_pairs={{4,0},{8,4},{12,8},{16,12},{20,16},{24,20},{28,24},{5,1},{9,5},{13... | collective-permute-start | bytes 221192 | tf_op jit(solution)/shard_map/ppermute | solution.py:18
  300.4 10.6 %copy-start.7 = (f32[8,32,384]{2,1,0:T(8,128)S(1)}, f32[8,32,384]{2,1,0:T(8,128)}, u32[]{:S(2)}) copy-start(f32[8,32,384]{2,1,0:T(8,128)} %get-tuple-element.51) | copy-start | bytes 1179652
  300.4 10.6 %copy-start.36 = (f32[384]{0:T(512)S(1)}, f32[384]{0:T(512)}, u32[]{:S(2)}) copy-start(f32[384]{0:T(512)} %param.9) | copy-start | bytes 4612
  300.5 6.5 %collective-permute-start.6 = (bf16[10,1,1152]{2,1,0:T(2,128)(2,1)S(1)}, bf16[10,1,1152]{2,1,0:T(2,128)(2,1)S(1)}, u32[]{:S(2)}, u32[]{:S(2)}) collective-permute-start(bf16[10,1,1152]{2,1,0:T(2,128)(2,1)S(1)} %get-tuple-element.40), channel_id=1, source_target_pairs={{1,0},{2,1},{3,2},{5,4},{6,5},{7,6},{9,8},{10,9},{11,10},{13,12},{... | collective-permute-start | bytes 69128 | tf_op jit(solution)/shard_map/ppermute | solution.py:18
  302.0 6.3 %collective-permute-start.7 = (bf16[10,1,1152]{2,1,0:T(2,128)(2,1)S(1)}, bf16[10,1,1152]{2,1,0:T(2,128)(2,1)S(1)}, u32[]{:S(2)}, u32[]{:S(2)}) collective-permute-start(bf16[10,1,1152]{2,1,0:T(2,128)(2,1)S(1)} %get-tuple-element.41), channel_id=1, source_target_pairs={{0,1},{1,2},{2,3},{4,5},{5,6},{6,7},{8,9},{9,10},{10,11},{12,13},{... | collective-permute-start | bytes 69128 | tf_op jit(solution)/shard_map/ppermute | solution.py:17
  311.1 45.7 %copy-start.19 = (bf16[8,32,384]{2,1,0:T(8,128)(2,1)S(1)}, bf16[8,32,384]{2,1,0:T(8,128)(2,1)}, u32[]{:S(2)}) copy-start(bf16[8,32,384]{2,1,0:T(8,128)(2,1)} %param.8) | copy-start | bytes 589828
  311.1 45.7 %copy-start.39 = (f32[256]{0:T(256)S(1)}, f32[256]{0:T(256)}, u32[]{:S(2)}) copy-start(f32[256]{0:T(256)} %rsqrt.22) | copy-start | bytes 3076
  (25 other events, 93.0 us)
Sparse Core Ops, SparseCore 0:
  93.4 128.7 all-reduce.5
where the time goes:
time: 366 us; the launch traced here: 365 us
  waiting for transfers between devices  139 us (38%)
  blocking collectives  125 us (34%)
  local copies, waits for them, and re-layouts  28.2 us (8%)
  other arithmetic  27.2 us (7%)
  starting transfers between devices  17.2 us (5%)
  between operations  14.7 us (4%)
  matrix products  13.3 us (4%)
    psum x1, waiting for transfers between devices, local(): lax.psum(jnp.einsum('phc,phd->hcd', queries * query_scale, keys_part * ke...  128 us
    psum x1, blocking collectives, local(): lax.psum((kernel_local, gain_local), ('rows', 'cols'))  43.8 us
    psum x1, blocking collectives, local(): lax.psum((query_squares, keys_squares), ('rows', 'cols'))  41.9 us
    psum x1, blocking collectives, local(): lax.psum((query_local, keys_local), ('rows', 'cols'))  39.7 us
    ppermute x4, starting transfers between devices, with_halo(): before = lax.ppermute(last, axis, up)  11.7 us
    ppermute x4, waiting for transfers between devices, with_halo(): after = lax.ppermute(leading, axis, down)  8.92 us
    unnamed x85, local copies, waits for them, and re-layouts  7.63 us
  transfers between devices with their start and end apart: 9, of which 6 were waited for; matrix products, arithmetic and copies ran while one was open for 1% of the time, Pallas kernels for 0%

commit v1 on v0

v1 whole, which is shorter than its diff:
```python
import functools

import jax
import jax.numpy as jnp
from jax import lax
from jax.experimental import pallas as pl
from jax.experimental.pallas import tpu as pltpu
from jax.sharding import PartitionSpec as P

norm_eps = 1e-05
unit_eps = 1e-06
HIGHEST = lax.Precision.HIGHEST
F32 = jnp.float32
BF16 = jnp.bfloat16
LANES = 128


def dot_exact(a, b, dims=((1,), (0,))):
    return lax.dot_general(a, b, (dims, ((), ())), precision=HIGHEST, preferred_element_type=F32)


def dot_bf16(a, b, dims=((1,), (0,))):
    return lax.dot_general(a, b, (dims, ((), ())), preferred_element_type=F32)


def ceil_to(value, step):
    return (value + step - 1) // step * step


def kernel(
    geo,
    x_ref,
    u_ref,
    gain_ref,
    proj_ref,
    taps_ref,
    sharp_ref,
    final_ref,
    out_ref,
    gain_out,
    taps_out,
    sharp_out,
    stage,
    col_in,
    corner_in,
    row_x,
    row_u,
    xe,
    ue,
    standard_ref,
    inv_ref,
    qkv,
    mixed,
    grad_out,
    grad_mixed,
    grad_qkv,
    pay1,
    part1,
    cols1,
    full1,
    pay2,
    part2,
    cols2,
    full2,
    halo_send,
    halo_recv,
    scatter_send,
    scatter_recv,
    cols_send,
    cols_recv,
    gather_send,
    gather_recv,
):
    R, C, H, B, ch, heads = geo
    hd = ch // heads
    c3 = 3 * ch
    W = B + 8
    row = lax.axis_index("rows")
    col = lax.axis_index("cols")
    up, down = lax.rem(row + R - 1, R), lax.rem(row + 1, R)
    left, right = lax.rem(col + C - 1, C), lax.rem(col + 1, C)
    MESH = pl.DeviceIdType.MESH

    barrier = pltpu.get_barrier_semaphore()

    def greet(r, c):
        pl.semaphore_signal(barrier, inc=1, device_id=(r, c), device_id_type=MESH)

    @pl.loop(1, R)
    def _(i):
        greet(lax.rem(row + i, R), col)

    @pl.loop(1, C)
    def _(i):
        greet(row, lax.rem(col + i, C))

    for r in (up, down):
        for c in (left, right):
            greet(r, c)

    xf = x_ref[...].astype(F32)
    uf = u_ref[...].astype(F32)
    stage[0, :, 0:2, :] = xf[:, 0:2, :]
    stage[0, :, 2:3, :] = uf[:, 0:1, :]
    stage[0, :, 3:4, :] = uf[:, 0:1, :]
    stage[1, :, 0:2, :] = xf[:, B - 2 : B, :]
    stage[1, :, 2:3, :] = uf[:, B - 1 : B, :]
    stage[1, :, 3:4, :] = uf[:, B - 1 : B, :]

    pl.semaphore_wait(barrier, (R - 1) + (C - 1) + 4)

    def send(n, src, dst, r, c):
        copy = pltpu.make_async_remote_copy(
            src_ref=src,
            dst_ref=dst,
            send_sem=halo_send.at[n],
            recv_sem=halo_recv.at[n],
            device_id=(r, c),
            device_id_type=MESH,
        )
        copy.start()
        return copy

    copies = [
        send(0, stage.at[0], col_in.at[1], row, left),
        send(1, stage.at[1], col_in.at[0], row, right),
        send(2, x_ref.at[pl.ds(0, 2)], row_x.at[1], up, col),
        send(3, x_ref.at[pl.ds(H - 2, 2)], row_x.at[0], down, col),
        send(4, u_ref.at[pl.ds(0, 1)], row_u.at[1], up, col),
        send(5, u_ref.at[pl.ds(H - 1, 1)], row_u.at[0], down, col),
        send(6, stage.at[0, pl.ds(0, 2)], corner_in.at[1, 1], up, left),
        send(7, stage.at[1, pl.ds(0, 2)], corner_in.at[1, 0], up, right),
        send(8, stage.at[0, pl.ds(H - 2, 2)], corner_in.at[0, 1], down, left),
        send(9, stage.at[1, pl.ds(H - 2, 2)], corner_in.at[0, 0], down, right),
    ]

    xe[2 : H + 2, 0:B, :] = xf
    xe[:, B:W, :] = jnp.zeros((H + 4, W - B, ch), F32)
    ue[1 : H + 1, 0:B, :] = uf
    ue[:, B:W, :] = jnp.zeros((H + 2, W - B, ch), F32)
    for copy in copies:
        copy.wait()
    xe[2 : H + 2, B : B + 2, :] = col_in[1, :, 0:2, :]
    xe[2 : H + 2, W - 2 : W, :] = col_in[0, :, 0:2, :]
    ue[1 : H + 1, B : B + 1, :] = col_in[1, :, 2:3, :]
    ue[1 : H + 1, W - 1 : W, :] = col_in[0, :, 2:3, :]
    for v, at in ((0, 0), (1, H + 2)):
        xe[at : at + 2, 0:B, :] = row_x[v].astype(F32)
        xe[at : at + 2, B : B + 2, :] = corner_in[v, 1, :, 0:2, :]
        xe[at : at + 2, W - 2 : W, :] = corner_in[v, 0, :, 0:2, :]
    for v, at, near in ((0, 0, 1), (1, H + 1, 0)):
        ue[at : at + 1, 0:B, :] = row_u[v].astype(F32)
        ue[at : at + 1, B : B + 1, :] = corner_in[v, 1, near : near + 1, 2:3, :]
        ue[at : at + 1, W - 1 : W, :] = corner_in[v, 0, near : near + 1, 2:3, :]

    def inside(width):
        shape = (H + 2 * width, W, LANES)
        i = row * H - width + lax.broadcasted_iota(jnp.int32, shape, 0)
        j = lax.broadcasted_iota(jnp.int32, shape, 1)
        near = j < B
        rim_right = (j >= B) & (j < B + width) & (col < C - 1)
        rim_left = (j >= W - width) & (col > 0)
        ok = (i >= 0) & (i < R * H) & (near | rim_right | rim_left)
        return jnp.where(ok, 1.0, 0.0).astype(F32)

    n2 = (H + 4) * W
    n1 = (H + 2) * W
    n0 = H * B
    feat = xe[...].reshape(n2, ch)
    centred = feat - jnp.mean(feat, axis=-1, keepdims=True)
    inv_std = lax.rsqrt(jnp.mean(centred * centred, axis=-1, keepdims=True) + norm_eps)
    standard = centred * inv_std
    standard_ref[...] = standard.reshape(H + 4, W, ch)[2 : H + 2, 0:B, :].reshape(n0, ch)
    inv_ref[...] = jnp.broadcast_to(
        inv_std.reshape(H + 4, W, 1)[2 : H + 2, 0:B, :].reshape(n0, 1), (n0, LANES)
    )
    mask2 = inside(2).reshape(n2, LANES)[:, 0:1] > 0.5
    normed = jnp.where(mask2, standard * gain_ref[...], 0.0).astype(BF16)
    qkv[...] = dot_bf16(normed, proj_ref[...]).astype(BF16).astype(F32).reshape(H + 4, W, c3)
    mask1 = inside(1).reshape(n1, LANES)[:, 0:1] > 0.5
    adjoint = jnp.where(mask1, ue[...].reshape(n1, ch), 0.0).astype(BF16)
    grad_out[...] = dot_bf16(adjoint, final_ref[...], ((1,), (1,)))

    def tap_rows(lanes):
        return [
            [taps_ref[a, :, lanes].astype(F32)[b : b + 1, :] for b in range(3)] for a in range(3)
        ]

    @pl.loop(0, c3 // LANES)
    def _(n):
        lanes = pl.ds(pl.multiple_of(n * LANES, LANES), LANES)
        taps = tap_rows(lanes)

        @pl.loop(0, H + 2)
        def _(i):
            window = [qkv[i + a, :, lanes] for a in range(3)]
            t = [sum(taps[a][b] * window[a] for a in range(3)) for b in range(3)]
            mixed[i, :, lanes] = t[1] + pltpu.roll(t[0], 1, 0) + pltpu.roll(t[2], W - 1, 0)

    def own(lo):
        return mixed[1 : H + 1, 0:B, lo : lo + ch].reshape(n0, ch)

    q, k, v = own(0), own(ch), own(2 * ch)
    g = grad_out[...].reshape(H + 2, W, ch)[1 : H + 1, 0:B, :].reshape(n0, ch)
    head_r = lax.broadcasted_iota(jnp.int32, (ch, ch), 0) // hd
    head_c = lax.broadcasted_iota(jnp.int32, (ch, ch), 1) // hd
    same_head = head_r == head_c
    along = ((0,), (0,))
    raw_gram = jnp.where(same_head, dot_exact(q, k, along), 0.0)
    raw_attn = jnp.where(same_head, dot_exact(g, v, along), 0.0)
    ones = jnp.ones((n0, LANES), F32)
    q_squares = dot_exact(q * q, ones, along)
    k_squares = dot_exact(k * k, ones, along)
    place_r = lax.rem(lax.broadcasted_iota(jnp.int32, (ch, LANES), 0), hd)
    place_c = lax.broadcasted_iota(jnp.int32, (ch, LANES), 1)
    fold_a = jnp.where(place_r == place_c, 1.0, 0.0).astype(F32)
    fold_b = jnp.where(place_r + hd == place_c, 1.0, 0.0).astype(F32)
    packed = dot_exact(raw_gram, fold_a) + dot_exact(raw_attn, fold_b)
    packed = jnp.where(place_c == 2 * hd, q_squares, packed)
    packed = jnp.where(place_c == 2 * hd + 1, k_squares, packed)
    size1 = pay1.shape[1]
    pay1[...] = pay_rows(packed, R * size1).reshape(R, size1, LANES)

    def reduce_all(stage_no, pay, part, cols, full):
        def rs(i):
            to = lax.rem(row + i, R)
            return pltpu.make_async_remote_copy(
                src_ref=pay.at[to],
                dst_ref=part.at[row],
                send_sem=scatter_send.at[stage_no, to],
                recv_sem=scatter_recv.at[stage_no, row],
                device_id=(to, col),
                device_id_type=MESH,
            )

        def rs_in(i):
            source = lax.rem(row + i, R)
            return pltpu.make_async_remote_copy(
                src_ref=pay.at[source],
                dst_ref=part.at[source],
                send_sem=scatter_send.at[stage_no, source],
                recv_sem=scatter_recv.at[stage_no, source],
                device_id=(source, col),
                device_id_type=MESH,
            )

        @pl.loop(1, R)
        def _(i):
            rs(i).start()

        part[row] = pay[row]

        @pl.loop(1, R)
        def _(i):
            rs_in(i).wait()

        total = part[0]
        for i in range(1, R):
            total = total + part[i]
        cols[col] = total

        def cs(i):
            to = lax.rem(col + i, C)
            return pltpu.make_async_remote_copy(
                src_ref=cols.at[col],
                dst_ref=cols.at[col],
                send_sem=cols_send.at[stage_no, to],
                recv_sem=cols_recv.at[stage_no, col],
                device_id=(row, to),
                device_id_type=MESH,
            )

        def cs_in(i):
            source = lax.rem(col + i, C)
            return pltpu.make_async_remote_copy(
                src_ref=cols.at[source],
                dst_ref=cols.at[source],
                send_sem=cols_send.at[stage_no, source],
                recv_sem=cols_recv.at[stage_no, source],
                device_id=(row, source),
                device_id_type=MESH,
            )

        @pl.loop(1, C)
        def _(i):
            cs(i).start()

        @pl.loop(1, C)
        def _(i):
            cs_in(i).wait()

        total = cols[0]
        for i in range(1, C):
            total = total + cols[i]
        full[row] = total

        def ag(i):
            to = lax.rem(row + i, R)
            return pltpu.make_async_remote_copy(
                src_ref=full.at[row],
                dst_ref=full.at[row],
                send_sem=gather_send.at[stage_no, to],
                recv_sem=gather_recv.at[stage_no, row],
                device_id=(to, col),
                device_id_type=MESH,
            )

        def ag_in(i):
            source = lax.rem(row + i, R)
            return pltpu.make_async_remote_copy(
                src_ref=full.at[source],
                dst_ref=full.at[source],
                send_sem=gather_send.at[stage_no, source],
                recv_sem=gather_recv.at[stage_no, source],
                device_id=(source, col),
                device_id_type=MESH,
            )

        @pl.loop(1, R)
        def _(i):
            ag(i).start()

        @pl.loop(1, R)
        def _(i):
            ag_in(i).wait()

    reduce_all(0, pay1, part1, cols1, full1)

    packed = full1[...].reshape(R * size1, LANES)[0:ch, :]
    q_scale = lax.rsqrt(packed[:, 2 * hd : 2 * hd + 1] + unit_eps)
    k_scale = lax.rsqrt(packed[:, 2 * hd + 1 : 2 * hd + 2] + unit_eps)
    diagonal = lax.broadcasted_iota(jnp.int32, (ch, ch), 0) == lax.broadcasted_iota(
        jnp.int32, (ch, ch), 1
    )

    def as_row(column):
        return jnp.sum(jnp.where(diagonal, column, 0.0), axis=0, keepdims=True)

    q_scale_row, k_scale_row = as_row(q_scale), as_row(k_scale)
    across = ((1,), (1,))
    gram = jnp.where(same_head, dot_exact(packed, fold_a, across), 0.0) * q_scale * k_scale_row
    grad_attn = jnp.where(same_head, dot_exact(packed, fold_b, across), 0.0)
    head_of = lax.broadcasted_iota(jnp.int32, (ch, 1), 0) // hd
    sharp = jnp.zeros((ch, 1), F32)
    for h in range(heads):
        sharp = jnp.where(head_of == h, sharp_ref[h], sharp)
    powers = jnp.where(same_head, jnp.exp(sharp * gram), 0.0)
    attention = powers / jnp.sum(powers, axis=-1, keepdims=True)
    scores = attention * (grad_attn - jnp.sum(attention * grad_attn, axis=-1, keepdims=True))
    pixels = R * C * n0
    per_channel = jnp.sum(scores * gram, axis=-1, keepdims=True)
    lane_head = lax.broadcasted_iota(jnp.int32, (ch, LANES), 1)
    row_head = lax.broadcasted_iota(jnp.int32, (ch, LANES), 0) // hd
    sharp_out[...] = (
        jnp.sum(jnp.where(lane_head == row_head, per_channel, 0.0), axis=0, keepdims=True) / pixels
    )
    grad_gram = sharp * scores
    q_dots = as_row(jnp.sum(grad_gram * gram, axis=-1, keepdims=True))
    k_dots = jnp.sum(grad_gram * gram, axis=0, keepdims=True)
    blend = q_scale * grad_gram * k_scale_row

    q_wide = mixed[:, :, 0:ch].reshape(n1, ch)
    k_wide = mixed[:, :, ch : 2 * ch].reshape(n1, ch)

    def keep(value, lo):
        value = jnp.where(mask1, value, 0.0).astype(BF16).astype(F32)
        grad_mixed[:, :, lo : lo + ch] = value.reshape(H + 2, W, ch)

    keep(dot_exact(k_wide, blend, across) - q_wide * (q_scale_row * q_scale_row * q_dots), 0)
    keep(dot_exact(q_wide, blend) - k_wide * (k_scale_row * k_scale_row * k_dots), ch)
    keep(dot_exact(grad_out[...], attention), 2 * ch)

    size2 = pay2.shape[0] // R
    pay2[...] = jnp.zeros_like(pay2)
    own_cols = lax.broadcasted_iota(jnp.int32, (W, LANES), 0) < B
    strips = W // 8

    @pl.loop(0, c3 // LANES)
    def _(n):
        lanes = pl.ds(pl.multiple_of(n * LANES, LANES), LANES)
        taps = tap_rows(lanes)

        def body(i, sums):
            grads = [grad_mixed[i + 2 - a, :, lanes] for a in range(3)]
            s = [sum(taps[a][b] * grads[a] for a in range(3)) for b in range(3)]
            value = s[1] + pltpu.roll(s[0], W - 1, 0) + pltpu.roll(s[2], 1, 0)
            grad_qkv[i, :, lanes] = value[0:B, :].astype(BF16)
            mid = jnp.where(own_cols, grads[1], 0.0)
            moved = [pltpu.roll(mid, W - 1, 0), mid, pltpu.roll(mid, 1, 0)]
            new = []
            for a in range(3):
                window = qkv[i + 1 + a, :, lanes]
                for b in range(3):
                    term = (window * moved[b]).reshape(strips, 8, LANES)
                    new.append(sums[3 * a + b] + jnp.sum(term, axis=0))
            return tuple(new)

        sums = lax.fori_loop(0, H, body, tuple(jnp.zeros((8, LANES), F32) for _ in range(9)))
        for t in range(9):
            pay2[pl.ds(n * 9 + t, 1), :] = jnp.sum(sums[t], axis=0, keepdims=True)

    grad_normed = dot_bf16(grad_qkv[...].reshape(n0, c3), proj_ref[...], across)
    standard = standard_ref[...]
    product = grad_normed * standard
    gain_sum = jnp.sum(product, axis=0, keepdims=True)
    base = 9 * (c3 // LANES)
    for n in range(ch // LANES):
        pay2[base + n : base + n + 1, :] = gain_sum[:, n * LANES : (n + 1) * LANES]
    scaled = grad_normed * gain_ref[...]
    slope = jnp.mean(scaled * standard, axis=-1, keepdims=True)
    grad_input = inv_ref[:, 0:1] * (
        scaled - jnp.mean(scaled, axis=-1, keepdims=True) - standard * slope
    )
    out_ref[...] = (u_ref[...].astype(F32) + grad_input.reshape(H, B, ch)).astype(BF16)

    reduce_all(
        1, pay2.reshape(R, size2, LANES), part2, cols2, full2
    )
    flat = full2[...].reshape(R * size2, LANES) / pixels
    for n in range(c3 // LANES):
        taps_out[:, n * LANES : (n + 1) * LANES] = flat[n * 9 : n * 9 + 9, :]
    for n in range(ch // LANES):
        gain_out[:, n * LANES : (n + 1) * LANES] = flat[base + n : base + n + 1, :]


def pay_rows(value, rows):
    if rows == value.shape[0]:
        return value
    fill = jnp.zeros((rows - value.shape[0], value.shape[1]), value.dtype)
    return jnp.concatenate([value, fill], axis=0)


def local(R, C, x, u, gain, proj, taps, sharp, final):
    H, B, ch = x.shape
    heads = sharp.shape[0]
    c3 = 3 * ch
    W = B + 8
    size1 = ceil_to(-(-ch // R), 8)
    rows2 = 9 * (c3 // LANES) + ch // LANES
    size2 = ceil_to(-(-rows2 // R), 8)
    vmem = pl.BlockSpec(memory_space=pltpu.VMEM)
    DMA = pltpu.SemaphoreType.DMA
    out, gain_sum, taps_sum, sharp_sum = pl.pallas_call(
        functools.partial(kernel, (R, C, H, B, ch, heads)),
        name="attention_backward",
        out_shape=(
            jax.ShapeDtypeStruct((H, B, ch), BF16),
            jax.ShapeDtypeStruct((1, ch), F32),
            jax.ShapeDtypeStruct((9, c3), F32),
            jax.ShapeDtypeStruct((1, LANES), F32),
        ),
        in_specs=[vmem] * 5 + [pl.BlockSpec(memory_space=pltpu.SMEM), vmem],
        out_specs=[vmem] * 4,
        scratch_shapes=[
            pltpu.VMEM((2, H, 4, ch), F32),
            pltpu.VMEM((2, H, 4, ch), F32),
            pltpu.VMEM((2, 2, 2, 4, ch), F32),
            pltpu.VMEM((2, 2, B, ch), BF16),
            pltpu.VMEM((2, 1, B, ch), BF16),
            pltpu.VMEM((H + 4, W, ch), F32),
            pltpu.VMEM((H + 2, W, ch), F32),
            pltpu.VMEM((H * B, ch), F32),
            pltpu.VMEM((H * B, LANES), F32),
            pltpu.VMEM((H + 4, W, c3), F32),
            pltpu.VMEM((H + 2, W, c3), F32),
            pltpu.VMEM(((H + 2) * W, ch), F32),
            pltpu.VMEM((H + 2, W, c3), F32),
            pltpu.VMEM((H, B, c3), BF16),
            pltpu.VMEM((R, size1, LANES), F32),
            pltpu.VMEM((R, size1, LANES), F32),
            pltpu.VMEM((C, size1, LANES), F32),
            pltpu.VMEM((R, size1, LANES), F32),
            pltpu.VMEM((R * size2, LANES), F32),
            pltpu.VMEM((R, size2, LANES), F32),
            pltpu.VMEM((C, size2, LANES), F32),
            pltpu.VMEM((R, size2, LANES), F32),
            DMA((10,)),
            DMA((10,)),
            DMA((2, R)),
            DMA((2, R)),
            DMA((2, C)),
            DMA((2, C)),
            DMA((2, R)),
            DMA((2, R)),
        ],
        compiler_params=pltpu.CompilerParams(
            collective_id=0, has_side_effects=True, vmem_limit_bytes=48 << 20
        ),
    )(x, u, gain.reshape(1, ch), proj, taps, sharp, final)
    return (out, gain_sum.reshape(ch), taps_sum.reshape(3, 3, c3), sharp_sum[0, :heads])


def solution(mesh):
    R, C = mesh.shape["rows"], mesh.shape["cols"]
    return jax.shard_map(
        functools.partial(local, R, C),
        mesh=mesh,
        in_specs=(P("rows", "cols", None), P("rows", "cols", None), P(), P(), P(), P(), P()),
        out_specs=(P("rows", "cols", None), P(), P(), P()),
        check_vma=False,
    )
```

time: 366 us -> 59.3 us (0.16)
  waiting for transfers between devices: 139 us -> 0 us
  blocking collectives: 125 us -> 0 us
  Pallas kernels: 0 us -> 50.5 us
  other arithmetic: 27.2 us -> 0.6 us
  local copies, waits for them, and re-layouts: 28.2 us -> 7.25 us
  starting transfers between devices: 17.2 us -> 0 us
  between operations: 14.7 us -> 0.65 us
  matrix products: 13.3 us -> 0 us
    psum x1 -> x0, waiting for transfers between devices: 128 us -> none  [local(): lax.psum(jnp.einsum('phc,phd->hcd', queries * query_scale, keys_part * ke...]
    psum x3 -> x0, blocking collectives: 125 us -> none  [the longest x1 43.8 us: local(): lax.psum((kernel_local, gain_local), ('rows', 'cols'))]
    pallas_call x0 -> x1, Pallas kernels: none -> 50.5 us  [local(): pl.pallas_call(functools.partial(kernel, (R, C, H, B, ch, heads)), name='...]
    ppermute x8 -> x0, starting transfers between devices: 17.1 us -> none  [the longest x4 11.7 us: with_halo(): before = lax.ppermute(last, axis, up)]
    dot_general x8 -> x0, matrix products: 13.3 us -> none  [the longest x1 3.27 us: local(): jnp.einsum('phd,hcd->phc', keys_unit, similarity_adjoint, precision=highest)]
    reduce_sum x9 -> x0, other arithmetic: 10.7 us -> none  [the longest x2 2.86 us: kernel_terms(): kernel_cols.append(jnp.sum(window * grad_f, axis=(0, 1)))]
    ppermute x8 -> x0, waiting for transfers between devices: 10.3 us -> none  [the longest x4 8.92 us: with_halo(): after = lax.ppermute(leading, axis, down)]
    convert_element_type x6 -> x0, other arithmetic: 8.64 us -> none  [the longest x1 2.79 us: local(): grad_qkv = conv_backward(grad_padded, taps, block_rows, block_cols).astyp...]
  transfers between devices with their start and end apart: 9 -> 0, of which waited for: 6 -> 0; matrix products, arithmetic and copies ran while one was open for 1% -> 0% of each run, Pallas kernels for 0% -> 0%
where the time goes in v1:
time: 59.3 us; the launch traced here: 59 us
  Pallas kernels  50.5 us (85%)
  local copies, waits for them, and re-layouts  7.25 us (12%)
  between operations  0.65 us (1%)
  other arithmetic  0.6 us (1%)
    pallas_call x1, Pallas kernels, local(): pl.pallas_call(functools.partial(kernel, (R, C, H, B, ch, heads)), name='...  50.5 us
    unnamed x13, local copies, waits for them, and re-layouts  5.41 us

profile of v1, /device:TPU:0, one launch (start us, length us, event | category | flops | bytes accessed | tf_op | source)
XLA Modules:
  0.0 59.0 jit_solution(6873105182398861876)
XLA Ops:
  0.6 0.0 copy-start.5
  0.6 0.7 %reshape.17.gain_ref = f32[1,384]{1,0:T(1,128)S(1)} reshape(f32[384]{0:T(512)} %param.9) | data formatting | bytes 3072 | tf_op jit(solution)/shard_map/reshape | solution.py:489
  1.3 0.0 copy-done.5
  1.3 0.0 copy-start
  1.3 1.2 %copy-done = bf16[384,1152]{1,0:T(8,128)(2,1)S(1)} copy-done((bf16[384,1152]{1,0:T(8,128)(2,1)S(1)}, bf16[384,1152]{1,0:T(8,128)(2,1)}, u32[]{:S(2)}) %copy-start) | copy-done | bytes 884760
  2.5 0.0 copy-start.1
  2.5 1.0 %copy-done.1 = bf16[384,384]{1,0:T(8,128)(2,1)S(1)} copy-done((bf16[384,384]{1,0:T(8,128)(2,1)S(1)}, bf16[384,384]{1,0:T(8,128)(2,1)}, u32[]{:S(2)}) %copy-start.1) | copy-done | bytes 294936
  3.5 0.0 copy-start.2
  3.5 0.9 %copy-done.2 = bf16[8,32,384]{2,1,0:T(8,128)(2,1)S(1)} copy-done((bf16[8,32,384]{2,1,0:T(8,128)(2,1)S(1)}, bf16[8,32,384]{2,1,0:T(8,128)(2,1)}, u32[]{:S(2)}) %copy-start.2) | copy-done | bytes 196632
  4.4 0.0 copy-start.3
  4.4 0.9 %copy-done.3 = bf16[8,32,384]{2,1,0:T(8,128)(2,1)S(1)} copy-done((bf16[8,32,384]{2,1,0:T(8,128)(2,1)S(1)}, bf16[8,32,384]{2,1,0:T(8,128)(2,1)}, u32[]{:S(2)}) %copy-start.3) | copy-done | bytes 196632
  5.3 0.0 copy-start.4
  5.3 0.7 %copy-done.4 = bf16[3,3,1152]{2,1,0:T(4,128)(2,1)S(1)} copy-done((bf16[3,3,1152]{2,1,0:T(4,128)(2,1)S(1)}, bf16[3,3,1152]{2,1,0:T(4,128)(2,1)}, u32[]{:S(2)}) %copy-start.4) | copy-done | bytes 20760
  6.1 50.5 %attention_backward.1 = (bf16[8,32,384]{2,1,0:T(8,128)(2,1)S(1)}, f32[1,384]{1,0:T(1,128)S(1)}, f32[9,1152]{1,0:T(8,128)S(1)}, f32[1,128]{1,0:T(1,128)S(1)}) custom-call(bf16[8,32,384]{2,1,0:T(8,128)(2,1)S(1)} %copy-done.2, bf16[8,32,384]{2,1,0:T(8,128)(2,1)S(1)} %copy-done.3, f32[1,384]{1,0:T(1,128)S(1)} %reshape.17.gain_ref, ...), custom_call_target="tpu_custom_call" | custom-call | tf_op jit(solution)/shard_map/attention_backward/pallas_call | solution.py:443
  56.5 0.5 slice_bitcast_fusion
  57.0 0.6 %reduce = f32[384]{0:T(512)} reduce(f32[1,384]{1,0:T(1,128)S(1)} %get-tuple-element.9, f32[]{:T(128)} %constant), dimensions={0}, to_apply=%get-tuple-element.9.reduce_sub_computation | reduce | bytes 3076 | tf_op jit(solution)/shard_map/attention_backward/pallas_call | solution.py:443
  57.6 0.6 %reshape.19 = f32[3,3,1152]{2,1,0:T(4,128)} reshape(f32[9,1152]{1,0:T(8,128)S(1)} %get-tuple-element.10) | data formatting | bytes 82944 | tf_op jit(solution)/shard_map/reshape | solution.py:490
  58.3 0.7 %copy.12 = bf16[8,32,384]{2,1,0:T(8,128)(2,1)} copy(bf16[8,32,384]{2,1,0:T(8,128)(2,1)S(1)} %get-tuple-element.16) | data formatting | bytes 393216
Async XLA Ops:
  0.6 0.7 %copy-start.5 = (f32[8]{0:T(128)S(1)}, f32[8]{0:T(128)}, u32[]{:S(2)}) copy-start(f32[8]{0:T(128)} %sharp_ref.1) | copy-start | bytes 100
  1.3 1.2 %copy-start = (bf16[384,1152]{1,0:T(8,128)(2,1)S(1)}, bf16[384,1152]{1,0:T(8,128)(2,1)}, u32[]{:S(2)}) copy-start(bf16[384,1152]{1,0:T(8,128)(2,1)} %proj_ref.1) | copy-start | bytes 2654212
  2.5 1.0 %copy-start.1 = (bf16[384,384]{1,0:T(8,128)(2,1)S(1)}, bf16[384,384]{1,0:T(8,128)(2,1)}, u32[]{:S(2)}) copy-start(bf16[384,384]{1,0:T(8,128)(2,1)} %final_ref.1) | copy-start | bytes 884740
  3.5 0.9 %copy-start.2 = (bf16[8,32,384]{2,1,0:T(8,128)(2,1)S(1)}, bf16[8,32,384]{2,1,0:T(8,128)(2,1)}, u32[]{:S(2)}) copy-start(bf16[8,32,384]{2,1,0:T(8,128)(2,1)} %x_ref.1) | copy-start | bytes 589828
  4.4 0.9 %copy-start.3 = (bf16[8,32,384]{2,1,0:T(8,128)(2,1)S(1)}, bf16[8,32,384]{2,1,0:T(8,128)(2,1)}, u32[]{:S(2)}) copy-start(bf16[8,32,384]{2,1,0:T(8,128)(2,1)} %u_ref.1) | copy-start | bytes 589828
  5.3 0.7 %copy-start.4 = (bf16[3,3,1152]{2,1,0:T(4,128)(2,1)S(1)}, bf16[3,3,1152]{2,1,0:T(4,128)(2,1)}, u32[]{:S(2)}) copy-start(bf16[3,3,1152]{2,1,0:T(4,128)(2,1)} %taps_ref.1) | copy-start | bytes 62212

commit v2 on v1

v2 whole, which is shorter than its diff:
```python
import functools

import jax
import jax.numpy as jnp
from jax import lax
from jax.experimental import pallas as pl
from jax.experimental.pallas import tpu as pltpu
from jax.sharding import PartitionSpec as P

norm_eps = 1e-05
unit_eps = 1e-06
F32 = jnp.float32
BF16 = jnp.bfloat16
LANES = 128


def dot_bf16(a, b, dims=((1,), (0,))):
    return lax.dot_general(a, b, (dims, ((), ())), preferred_element_type=F32)


def ceil_to(value, step):
    return (value + step - 1) // step * step


def halves(a):
    high = a.astype(BF16)
    return high, (a - high.astype(F32)).astype(BF16)


def dot_split(a, b, dims=((1,), (0,))):
    return dot_bf16(a[0], b[0], dims) + (dot_bf16(a[0], b[1], dims) + dot_bf16(a[1], b[0], dims))


def kernel(
    geo,
    x_hbm,
    u_hbm,
    gain_hbm,
    proj_hbm,
    taps_hbm,
    sharp_ref,
    final_hbm,
    out_hbm,
    gain_out,
    taps_out,
    sharp_out,
    x_ref,
    u_ref,
    gain_ref,
    proj_ref,
    taps_ref,
    final_ref,
    out_ref,
    load_sem,
    stage,
    col_in,
    corner_in,
    row_x,
    row_u,
    rim_x,
    side_x,
    rim_u,
    side_u,
    standard_ref,
    inv_ref,
    qkv,
    mixed,
    grad_out,
    grad_mixed,
    grad_qkv,
    split,
    pay1,
    part1,
    cols1,
    full1,
    pay2,
    part2,
    cols2,
    full2,
    gain_all,
    gain_cols,
    halo_send,
    halo_recv,
    red_send,
    red_recv,
):
    R, C, H, B, ch, heads = geo
    hd = ch // heads
    c3 = 3 * ch
    W = B + 8
    S = W - B
    row = lax.axis_index("rows")
    col = lax.axis_index("cols")
    up, down = lax.rem(row + R - 1, R), lax.rem(row + 1, R)
    left, right = lax.rem(col + C - 1, C), lax.rem(col + 1, C)
    MESH = pl.DeviceIdType.MESH

    barrier = pltpu.get_barrier_semaphore()

    def greet(r, c):
        pl.semaphore_signal(barrier, inc=1, device_id=(r, c), device_id_type=MESH)

    for i in range(1, R):
        greet(lax.rem(row + i, R), col)
    for i in range(1, C):
        greet(row, lax.rem(col + i, C))
    for r in (up, down):
        for c in (left, right):
            greet(r, c)

    loads = [
        pltpu.make_async_copy(src, dst, load_sem.at[n])
        for n, (src, dst) in enumerate(
            (
                (x_hbm, x_ref),
                (u_hbm, u_ref),
                (gain_hbm, gain_ref.at[0]),
                (proj_hbm, proj_ref),
                (final_hbm, final_ref),
                (taps_hbm, taps_ref),
            )
        )
    ]
    for load in loads:
        load.start()
    loads[0].wait()
    loads[1].wait()
    xf = x_ref[...].astype(F32)
    uf = u_ref[...].astype(F32)
    stage[0, :, 0:2, :] = xf[:, 0:2, :]
    stage[0, :, 2:3, :] = uf[:, 0:1, :]
    stage[0, :, 3:4, :] = uf[:, 0:1, :]
    stage[1, :, 0:2, :] = xf[:, B - 2 : B, :]
    stage[1, :, 2:3, :] = uf[:, B - 1 : B, :]
    stage[1, :, 3:4, :] = uf[:, B - 1 : B, :]

    pl.semaphore_wait(barrier, (R - 1) + (C - 1) + 4)

    def send(n, src, dst, r, c):
        pltpu.make_async_remote_copy(
            src_ref=src,
            dst_ref=dst,
            send_sem=halo_send.at[n],
            recv_sem=halo_recv.at[n],
            device_id=(r, c),
            device_id_type=MESH,
        ).start()

    send(0, stage.at[0], col_in.at[1], row, left)
    send(0, stage.at[1], col_in.at[0], row, right)
    send(1, stage.at[0, pl.ds(0, 2)], corner_in.at[1, 1], up, left)
    send(1, stage.at[1, pl.ds(0, 2)], corner_in.at[1, 0], up, right)
    send(1, stage.at[0, pl.ds(H - 2, 2)], corner_in.at[0, 1], down, left)
    send(1, stage.at[1, pl.ds(H - 2, 2)], corner_in.at[0, 0], down, right)
    send(2, x_ref.at[pl.ds(0, 2)], row_x.at[1], up, col)
    send(2, x_ref.at[pl.ds(H - 2, 2)], row_x.at[0], down, col)
    send(3, u_ref.at[pl.ds(0, 1)], row_u.at[1], up, col)
    send(3, u_ref.at[pl.ds(H - 1, 1)], row_u.at[0], down, col)

    def halo_copy(n, buf):
        return pltpu.make_async_remote_copy(
            src_ref=buf,
            dst_ref=buf,
            send_sem=halo_send.at[n],
            recv_sem=halo_recv.at[n],
            device_id=(row, left),
            device_id_type=MESH,
        )

    n0 = H * B
    across = ((1,), (1,))

    def normalise(feat):
        centred = feat - jnp.mean(feat, axis=-1, keepdims=True)
        inv_std = lax.rsqrt(jnp.mean(centred * centred, axis=-1, keepdims=True) + norm_eps)
        return centred * inv_std, inv_std

    def project(normed):
        return dot_bf16(normed.astype(BF16), proj_ref[...]).astype(BF16).astype(F32)

    loads[2].wait()
    loads[3].wait()
    standard, inv_std = normalise(xf.reshape(n0, ch))
    standard_ref[...] = standard
    inv_ref[...] = jnp.broadcast_to(inv_std, (n0, LANES))
    qkv[2 : H + 2, 0:B, :] = project(standard * gain_ref[...]).reshape(H, B, c3)
    loads[4].wait()
    loads[5].wait()
    grad_out[1 : H + 1, 0:B, :] = dot_bf16(
        u_ref[...].reshape(n0, ch), final_ref[...], across
    ).reshape(H, B, ch)

    rim_x[:, B:W, :] = jnp.zeros((4, S, ch), F32)
    side_x[...] = jnp.zeros((H, S, ch), F32)
    rim_u[:, B:W, :] = jnp.zeros((2, S, ch), F32)
    side_u[...] = jnp.zeros((H, S, ch), F32)
    halo_copy(0, col_in).wait_recv()
    halo_copy(1, corner_in).wait_recv()
    halo_copy(2, row_x).wait_recv()
    halo_copy(3, row_u).wait_recv()
    side_x[:, 0:2, :] = col_in[1, :, 0:2, :]
    side_x[:, S - 2 : S, :] = col_in[0, :, 0:2, :]
    for v in (0, 1):
        at = 2 * v
        rim_x[at : at + 2, 0:B, :] = row_x[v].astype(F32)
        rim_x[at : at + 2, B : B + 2, :] = corner_in[v, 1, :, 0:2, :]
        rim_x[at : at + 2, W - 2 : W, :] = corner_in[v, 0, :, 0:2, :]

    def inside(shape, i, first_col, width):
        j = first_col + lax.broadcasted_iota(jnp.int32, shape, 1)
        rim_right = (j >= B) & (j < B + width) & (col < C - 1)
        rim_left = (j >= W - width) & (col > 0)
        ok = (i >= 0) & (i < R * H) & ((j < B) | rim_right | rim_left)
        return jnp.where(ok, 1.0, 0.0).astype(F32).reshape(-1, LANES)[:, 0:1] > 0.5

    def plane(shape):
        return lax.broadcasted_iota(jnp.int32, shape, 0)

    n_rim, n_side = 4 * W, H * S
    plane4 = plane((4, W, LANES))
    rim_rows = row * H + jnp.where(plane4 < 2, plane4 - 2, plane4 + H - 2)
    rim_ok = inside((4, W, LANES), rim_rows, 0, 2)
    side_ok = inside((H, S, LANES), row * H + plane((H, S, LANES)), B, 2)
    rim_norm = normalise(rim_x[...].reshape(n_rim, ch))[0] * gain_ref[...]
    side_norm = normalise(side_x[...].reshape(n_side, ch))[0] * gain_ref[...]
    rim_qkv = project(
        jnp.concatenate([jnp.where(rim_ok, rim_norm, 0.0), jnp.where(side_ok, side_norm, 0.0)], 0)
    )
    qkv[0:2, :, :] = rim_qkv[0 : 2 * W].reshape(2, W, c3)
    qkv[H + 2 : H + 4, :, :] = rim_qkv[2 * W : n_rim].reshape(2, W, c3)
    qkv[2 : H + 2, B:W, :] = rim_qkv[n_rim:].reshape(H, S, c3)

    def tap_rows(lanes):
        return [
            [taps_ref[a, :, lanes].astype(F32)[b : b + 1, :] for b in range(3)] for a in range(3)
        ]

    def lanes_of(n):
        return pl.ds(pl.multiple_of(n * LANES, LANES), LANES)

    def mix(taps, lanes, i):
        window = [qkv[i + a, :, lanes] for a in range(3)]
        t = [sum(taps[a][b] * window[a] for a in range(3)) for b in range(3)]
        mixed[i, :, lanes] = t[1] + pltpu.roll(t[0], 1, 0) + pltpu.roll(t[2], W - 1, 0)

    @pl.loop(0, c3 // LANES)
    def _(n):
        taps = tap_rows(lanes_of(n))
        for i in range(1, H + 1):
            mix(taps, lanes_of(n), i)

    def own(lo):
        return mixed[1 : H + 1, 0:B, lo : lo + ch].reshape(n0, ch)

    q, k, v = own(0), own(ch), own(2 * ch)
    g = grad_out[1 : H + 1, 0:B, :].reshape(n0, ch)
    head_r = lax.broadcasted_iota(jnp.int32, (ch, ch), 0) // hd
    head_c = lax.broadcasted_iota(jnp.int32, (ch, ch), 1) // hd
    same_head = head_r == head_c
    diagonal = lax.broadcasted_iota(jnp.int32, (ch, ch), 0) == lax.broadcasted_iota(
        jnp.int32, (ch, ch), 1
    )
    along = ((0,), (0,))

    def as_column(line):
        return jnp.sum(jnp.where(diagonal, line, 0.0), axis=1, keepdims=True)

    def as_row(column):
        return jnp.sum(jnp.where(diagonal, column, 0.0), axis=0, keepdims=True)

    raw_gram = jnp.where(same_head, dot_split(halves(q), halves(k), along), 0.0)
    raw_attn = jnp.where(same_head, dot_split(halves(g), halves(v), along), 0.0)
    q_squares = as_column(jnp.sum(q * q, axis=0, keepdims=True))
    k_squares = as_column(jnp.sum(k * k, axis=0, keepdims=True))
    place_r = lax.rem(lax.broadcasted_iota(jnp.int32, (ch, LANES), 0), hd)
    place_c = lax.broadcasted_iota(jnp.int32, (ch, LANES), 1)
    fold_a = jnp.where(place_r == place_c, 1.0, 0.0).astype(BF16)
    fold_b = jnp.where(place_r + hd == place_c, 1.0, 0.0).astype(BF16)

    def thirds(a):
        high, low = halves(a)
        return high, low, (a - high.astype(F32) - low.astype(F32)).astype(BF16)

    def fold(a, matrix, dims=((1,), (0,))):
        return sum(dot_bf16(part, matrix, dims) for part in thirds(a))

    packed = fold(raw_gram, fold_a) + fold(raw_attn, fold_b)
    packed = jnp.where(place_c == 2 * hd, q_squares, packed)
    packed = jnp.where(place_c == 2 * hd + 1, k_squares, packed)
    size1 = pay1.shape[1]
    pay1[...] = pay_rows(packed, R * size1).reshape(R, size1, LANES)

    def copy_to(phase, src, dst, r, c):
        return pltpu.make_async_remote_copy(
            src_ref=src,
            dst_ref=dst,
            send_sem=red_send.at[phase],
            recv_sem=red_recv.at[phase],
            device_id=(r, c),
            device_id_type=MESH,
        )

    def arrive(phase, buf, count):
        some = buf.at[pl.ds(0, count)]
        copy_to(phase, some, some, row, left).wait_recv()

    def left_here(phase, buf, count):
        some = buf.at[pl.ds(0, count)]
        copy_to(phase, some, some, row, left).wait_send()

    def scatter(phase, pay, part):
        for i in range(1, R):
            to = lax.rem(row + i, R)
            copy_to(phase, pay.at[to], part.at[i - 1], to, col).start()

    def scattered(phase, pay, part):
        arrive(phase, part, R - 1)
        total = pay[row]
        for i in range(R - 1):
            total = total + part[i]
        return total

    def to_cols(phase, cols, value):
        cols[col] = value
        for i in range(1, C):
            to = lax.rem(col + i, C)
            copy_to(phase, cols.at[col], cols.at[col], row, to).start()

    def summed(phase, buf, count):
        arrive(phase, buf, count - 1)
        total = buf[0]
        for i in range(1, count):
            total = total + buf[i]
        return total

    def to_rows(phase, full, value):
        full[row] = value
        for i in range(1, R):
            to = lax.rem(row + i, R)
            copy_to(phase, full.at[row], full.at[row], to, col).start()

    scatter(0, pay1, part1)

    @pl.loop(0, c3 // LANES)
    def _(n):
        taps = tap_rows(lanes_of(n))
        for i in (0, H + 1):
            mix(taps, lanes_of(n), i)

    side_u[:, 0:1, :] = col_in[1, :, 2:3, :]
    side_u[:, S - 1 : S, :] = col_in[0, :, 2:3, :]
    for v, near in ((0, 1), (1, 0)):
        rim_u[v : v + 1, 0:B, :] = row_u[v].astype(F32)
        rim_u[v : v + 1, B : B + 1, :] = corner_in[v, 1, near : near + 1, 2:3, :]
        rim_u[v : v + 1, W - 1 : W, :] = corner_in[v, 0, near : near + 1, 2:3, :]
    n1 = (H + 2) * W
    rows1 = row * H - 1 + plane((H + 2, W, LANES))
    mask1 = inside((H + 2, W, LANES), rows1, 0, 1)
    rim_adjoint = jnp.concatenate(
        [rim_u[...].reshape(2 * W, ch), side_u[...].reshape(n_side, ch)], 0
    ).astype(BF16)
    rim_out = dot_bf16(rim_adjoint, final_ref[...], across)
    grad_out[0:1, :, :] = rim_out[0:W].reshape(1, W, ch)
    grad_out[H + 1 : H + 2, :, :] = rim_out[W : 2 * W].reshape(1, W, ch)
    grad_out[1 : H + 1, B:W, :] = rim_out[2 * W :].reshape(H, S, ch)
    for n, wide in enumerate((mixed[:, :, 0:ch], mixed[:, :, ch : 2 * ch], grad_out[...])):
        split[2 * n], split[2 * n + 1] = halves(wide.reshape(n1, ch))

    to_cols(1, cols1, scattered(0, pay1, part1))
    to_rows(2, full1, summed(1, cols1, C))
    arrive(2, full1, R - 1)

    packed = full1[...].reshape(R * size1, LANES)[0:ch, :]
    q_scale = lax.rsqrt(packed[:, 2 * hd : 2 * hd + 1] + unit_eps)
    k_scale = lax.rsqrt(packed[:, 2 * hd + 1 : 2 * hd + 2] + unit_eps)
    q_scale_row, k_scale_row = as_row(q_scale), as_row(k_scale)
    gram = jnp.where(same_head, fold(packed, fold_a, across), 0.0) * q_scale * k_scale_row
    grad_attn = jnp.where(same_head, fold(packed, fold_b, across), 0.0)
    head_of = lax.broadcasted_iota(jnp.int32, (ch, 1), 0) // hd
    sharp = jnp.zeros((ch, 1), F32)
    for h in range(heads):
        sharp = jnp.where(head_of == h, sharp_ref[h], sharp)
    powers = jnp.where(same_head, jnp.exp(sharp * gram), 0.0)
    attention = powers / jnp.sum(powers, axis=-1, keepdims=True)
    scores = attention * (grad_attn - jnp.sum(attention * grad_attn, axis=-1, keepdims=True))
    pixels = R * C * n0
    weighted = scores * gram
    per_channel = jnp.sum(weighted, axis=-1, keepdims=True)
    row_head = lax.broadcasted_iota(jnp.int32, (ch, LANES), 0) // hd
    sharp_out[...] = (
        jnp.sum(jnp.where(place_c == row_head, per_channel, 0.0), axis=0, keepdims=True) / pixels
    )
    q_dots = as_row(sharp * per_channel)
    k_dots = jnp.sum(sharp * weighted, axis=0, keepdims=True)
    blend = halves(q_scale * (sharp * scores) * k_scale_row)

    def keep(value, lo):
        value = jnp.where(mask1, value, 0.0).astype(BF16).astype(F32)
        grad_mixed[:, :, lo : lo + ch] = value.reshape(H + 2, W, ch)

    q_pair, k_pair, g_pair = [(split[2 * n], split[2 * n + 1]) for n in range(3)]
    q_wide = mixed[:, :, 0:ch].reshape(n1, ch)
    k_wide = mixed[:, :, ch : 2 * ch].reshape(n1, ch)
    keep(dot_split(k_pair, blend, across) - q_wide * (q_scale_row * q_scale_row * q_dots), 0)
    keep(dot_split(q_pair, blend) - k_wide * (k_scale_row * k_scale_row * k_dots), ch)
    keep(dot_split(g_pair, halves(attention)), 2 * ch)

    size2 = pay2.shape[0] // R
    used2 = 9 * (c3 // LANES)
    pay2[used2:, :] = jnp.zeros((R * size2 - used2, LANES), F32)
    own_cols = lax.broadcasted_iota(jnp.int32, (W, LANES), 0) < B
    strips = W // 8

    @pl.loop(0, c3 // LANES)
    def _(n):
        lanes = lanes_of(n)

        def body(i, sums):
            mid = jnp.where(own_cols, grad_mixed[i + 1, :, lanes], 0.0)
            moved = [pltpu.roll(mid, W - 1, 0), mid, pltpu.roll(mid, 1, 0)]
            new = []
            for a in range(3):
                window = qkv[i + 1 + a, :, lanes]
                for b in range(3):
                    term = (window * moved[b]).reshape(strips, 8, LANES)
                    new.append(sums[3 * a + b] + jnp.sum(term, axis=0))
            return tuple(new)

        sums = tuple(jnp.zeros((8, LANES), F32) for _ in range(9))
        sums = lax.fori_loop(0, H, body, sums, unroll=True)
        for t in range(9):
            pay2[pl.ds(n * 9 + t, 1), :] = jnp.sum(sums[t], axis=0, keepdims=True)

    pay2_parts = pay2.reshape(R, size2, LANES)
    scatter(3, pay2_parts, part2)

    @pl.loop(0, c3 // LANES)
    def _(n):
        lanes = lanes_of(n)
        taps = tap_rows(lanes)
        for i in range(H):
            grads = [grad_mixed[i + 2 - a, :, lanes] for a in range(3)]
            s = [sum(taps[a][b] * grads[a] for a in range(3)) for b in range(3)]
            value = s[1] + pltpu.roll(s[0], W - 1, 0) + pltpu.roll(s[2], 1, 0)
            grad_qkv[i, :, lanes] = value[0:B, :].astype(BF16)

    to_cols(4, cols2, scattered(3, pay2_parts, part2))

    grad_normed = dot_bf16(grad_qkv[...].reshape(n0, c3), proj_ref[...], across)
    standard = standard_ref[...]
    gain_sum = jnp.sum(grad_normed * standard, axis=0, keepdims=True)
    gain_rows = [gain_sum[:, n * LANES : (n + 1) * LANES] for n in range(ch // LANES)]
    gain_rows += [jnp.zeros((gain_all.shape[1] - len(gain_rows), LANES), F32)]
    to_rows(5, gain_all, jnp.concatenate(gain_rows, 0))
    to_rows(6, full2, summed(4, cols2, C))

    scaled = grad_normed * gain_ref[...]
    slope = jnp.mean(scaled * standard, axis=-1, keepdims=True)
    grad_input = inv_ref[:, 0:1] * (
        scaled - jnp.mean(scaled, axis=-1, keepdims=True) - standard * slope
    )
    out_ref[...] = (u_ref[...].astype(F32) + grad_input.reshape(H, B, ch)).astype(BF16)
    store = pltpu.make_async_copy(out_ref, out_hbm, load_sem.at[6])
    store.start()

    to_cols(7, gain_cols, summed(5, gain_all, R))
    arrive(6, full2, R - 1)
    flat = full2[...].reshape(R * size2, LANES) / pixels
    for n in range(c3 // LANES):
        taps_out[:, n * LANES : (n + 1) * LANES] = flat[n * 9 : n * 9 + 9, :]
    gain_total = summed(7, gain_cols, C) / pixels
    for n in range(ch // LANES):
        gain_out[:, n * LANES : (n + 1) * LANES] = gain_total[n : n + 1, :]
    store.wait()
    for n, buf in enumerate((col_in, corner_in, row_x, row_u)):
        halo_copy(n, buf).wait_send()
    sent = (
        (0, part1, R),
        (1, cols1, C),
        (2, full1, R),
        (3, part2, R),
        (4, cols2, C),
        (5, gain_all, R),
        (6, full2, R),
        (7, gain_cols, C),
    )
    for phase, buf, count in sent:
        left_here(phase, buf, count - 1)


def pay_rows(value, rows):
    if rows == value.shape[0]:
        return value
    fill = jnp.zeros((rows - value.shape[0], value.shape[1]), value.dtype)
    return jnp.concatenate([value, fill], axis=0)


def local(R, C, x, u, gain, proj, taps, sharp, final):
    H, B, ch = x.shape
    heads = sharp.shape[0]
    c3 = 3 * ch
    W = B + 8
    size1 = ceil_to(-(-ch // R), 8)
    rows2 = 9 * (c3 // LANES)
    S = W - B
    size3 = ceil_to(ch // LANES, 8)
    size2 = ceil_to(-(-rows2 // R), 8)
    vmem = pl.BlockSpec(memory_space=pltpu.VMEM)
    hbm = pl.BlockSpec(memory_space=pltpu.HBM)
    DMA = pltpu.SemaphoreType.DMA
    out, gain_sum, taps_sum, sharp_sum = pl.pallas_call(
        functools.partial(kernel, (R, C, H, B, ch, heads)),
        name="attention_backward",
        out_shape=(
            jax.ShapeDtypeStruct((H, B, ch), BF16),
            jax.ShapeDtypeStruct((1, ch), F32),
            jax.ShapeDtypeStruct((9, c3), F32),
            jax.ShapeDtypeStruct((1, LANES), F32),
        ),
        in_specs=[hbm] * 5 + [pl.BlockSpec(memory_space=pltpu.SMEM), hbm],
        out_specs=[hbm] + [vmem] * 3,
        scratch_shapes=[
            pltpu.VMEM((H, B, ch), BF16),
            pltpu.VMEM((H, B, ch), BF16),
            pltpu.VMEM((1, ch), F32),
            pltpu.VMEM((ch, c3), BF16),
            pltpu.VMEM((3, 3, c3), BF16),
            pltpu.VMEM((ch, ch), BF16),
            pltpu.VMEM((H, B, ch), BF16),
            DMA((7,)),
            pltpu.VMEM((2, H, 4, ch), F32),
            pltpu.VMEM((2, H, 4, ch), F32),
            pltpu.VMEM((2, 2, 2, 4, ch), F32),
            pltpu.VMEM((2, 2, B, ch), BF16),
            pltpu.VMEM((2, 1, B, ch), BF16),
            pltpu.VMEM((4, W, ch), F32),
            pltpu.VMEM((H, S, ch), F32),
            pltpu.VMEM((2, W, ch), F32),
            pltpu.VMEM((H, S, ch), F32),
            pltpu.VMEM((H * B, ch), F32),
            pltpu.VMEM((H * B, LANES), F32),
            pltpu.VMEM((H + 4, W, c3), F32),
            pltpu.VMEM((H + 2, W, c3), F32),
            pltpu.VMEM((H + 2, W, ch), F32),
            pltpu.VMEM((H + 2, W, c3), F32),
            pltpu.VMEM((H, B, c3), BF16),
            pltpu.VMEM((6, (H + 2) * W, ch), BF16),
            pltpu.VMEM((R, size1, LANES), F32),
            pltpu.VMEM((R - 1, size1, LANES), F32),
            pltpu.VMEM((C, size1, LANES), F32),
            pltpu.VMEM((R, size1, LANES), F32),
            pltpu.VMEM((R * size2, LANES), F32),
            pltpu.VMEM((R - 1, size2, LANES), F32),
            pltpu.VMEM((C, size2, LANES), F32),
            pltpu.VMEM((R, size2, LANES), F32),
            pltpu.VMEM((R, size3, LANES), F32),
            pltpu.VMEM((C, size3, LANES), F32),
            DMA((4,)),
            DMA((4,)),
            DMA((8,)),
            DMA((8,)),
        ],
        compiler_params=pltpu.CompilerParams(
            collective_id=0, has_side_effects=True, vmem_limit_bytes=56203673
        ),
    )(x, u, gain, proj, taps, sharp, final)
    return (out, gain_sum.reshape(ch), taps_sum.reshape(3, 3, c3), sharp_sum[0, :heads])


def solution(mesh):
    R, C = mesh.shape["rows"], mesh.shape["cols"]
    return jax.shard_map(
        functools.partial(local, R, C),
        mesh=mesh,
        in_specs=(P("rows", "cols", None), P("rows", "cols", None), P(), P(), P(), P(), P()),
        out_specs=(P("rows", "cols", None), P(), P(), P()),
        check_vma=False,
    )
```

time: 59.3 us -> 49.3 us (0.83)
  Pallas kernels: 50.5 us -> 43.9 us
  local copies, waits for them, and re-layouts: 7.25 us -> 3.91 us
    pallas_call x1, Pallas kernels: 50.5 us -> 43.9 us  [local(): pl.pallas_call(functools.partial(kernel, (R, C, H, B, ch, heads)), name='...]
    unnamed x13 -> x7, local copies, waits for them, and re-layouts: 5.41 us -> 2.75 us
    reshape x1 -> x0, local copies, waits for them, and re-layouts: 0.69 us -> none  [local(): gain.reshape(1, ch)]
where the time goes in v2:
time: 49.3 us; the launch traced here: 49 us
  Pallas kernels  43.9 us (89%)
  local copies, waits for them, and re-layouts  3.91 us (8%)
  between operations  0.65 us (1%)
  other arithmetic  0.6 us (1%)
    pallas_call x1, Pallas kernels, local(): pl.pallas_call(functools.partial(kernel, (R, C, H, B, ch, heads)), name='...  43.9 us
    unnamed x7, local copies, waits for them, and re-layouts  2.75 us

profile of v2, /device:TPU:0, one launch (start us, length us, event | category | flops | bytes accessed | tf_op | source)
XLA Modules:
  0.0 49.0 jit_solution(6421942072089913169)
XLA Ops:
  0.6 0.0 copy-start
  0.6 0.7 %copy-done = bf16[3,3,1152]{2,1,0:T(4,128)(2,1)S(1)} copy-done((bf16[3,3,1152]{2,1,0:T(4,128)(2,1)S(1)}, bf16[3,3,1152]{2,1,0:T(4,128)(2,1)}, u32[]{:S(2)}) %copy-start) | copy-done | bytes 20760
  1.4 0.0 copy-start.1
  1.4 0.7 %copy-done.1 = f32[384]{0:T(512)S(1)} copy-done((f32[384]{0:T(512)S(1)}, f32[384]{0:T(512)}, u32[]{:S(2)}) %copy-start.1) | copy-done | bytes 1560
  2.1 0.0 copy-start.2
  2.1 0.7 %copy-done.2 = f32[8]{0:T(128)S(1)} copy-done((f32[8]{0:T(128)S(1)}, f32[8]{0:T(128)}, u32[]{:S(2)}) %copy-start.2) | copy-done | bytes 56
  2.7 43.9 %attention_backward.1 = (bf16[8,32,384]{2,1,0:T(8,128)(2,1)S(1)}, f32[1,384]{1,0:T(1,128)S(1)}, f32[9,1152]{1,0:T(8,128)S(1)}, f32[1,128]{1,0:T(1,128)S(1)}) custom-call(bf16[8,32,384]{2,1,0:T(8,128)(2,1)} %x_hbm.1, bf16[8,32,384]{2,1,0:T(8,128)(2,1)} %u_hbm.1, f32[384]{0:T(512)S(1)} %copy-done.1, bf16[384,1152]{1,0:T(8,128)(2,1)} %proj_hbm.1, ...), custom_call_target="tpu_custom_call" | custom-call | tf_op jit(solution)/shard_map/attention_backward/pallas_call | solution.py:511
  46.6 0.5 %slice_bitcast_fusion = f32[8]{0:T(128)} fusion(f32[1,128]{1,0:T(1,128)S(1)} %get-tuple-element.11), kind=kLoop, calls=%fused_computation | loop fusion | bytes 64 | tf_op jit(solution)/shard_map/squeeze | solution.py:567
  47.1 0.6 %reduce = f32[384]{0:T(512)} reduce(f32[1,384]{1,0:T(1,128)S(1)} %get-tuple-element.9, f32[]{:T(128)} %constant), dimensions={0}, to_apply=%get-tuple-element.9.reduce_sub_computation | reduce | bytes 3076 | tf_op jit(solution)/shard_map/attention_backward/pallas_call | solution.py:511
  47.7 0.6 %reshape.15 = f32[3,3,1152]{2,1,0:T(4,128)} reshape(f32[9,1152]{1,0:T(8,128)S(1)} %get-tuple-element.10) | data formatting | bytes 82944 | tf_op jit(solution)/shard_map/reshape | solution.py:567
  48.4 0.7 %copy.12 = bf16[8,32,384]{2,1,0:T(8,128)(2,1)} copy(bf16[8,32,384]{2,1,0:T(8,128)(2,1)S(1)} %get-tuple-element.16) | data formatting | bytes 393216
Async XLA Ops:
  0.6 0.7 %copy-start = (bf16[3,3,1152]{2,1,0:T(4,128)(2,1)S(1)}, bf16[3,3,1152]{2,1,0:T(4,128)(2,1)}, u32[]{:S(2)}) copy-start(bf16[3,3,1152]{2,1,0:T(4,128)(2,1)} %taps_hbm.1) | copy-start | bytes 62212
  1.4 0.7 %copy-start.1 = (f32[384]{0:T(512)S(1)}, f32[384]{0:T(512)}, u32[]{:S(2)}) copy-start(f32[384]{0:T(512)} %gain_hbm.1) | copy-start | bytes 4612
  2.1 0.7 %copy-start.2 = (f32[8]{0:T(128)S(1)}, f32[8]{0:T(128)}, u32[]{:S(2)}) copy-start(f32[8]{0:T(128)} %sharp_ref.1) | copy-start | bytes 100

commit v3 on v2

--- a/solution.py
+++ b/solution.py
@@ -493,6 +493,10 @@
         return value
     fill = jnp.zeros((rows - value.shape[0], value.shape[1]), value.dtype)
     return jnp.concatenate([value, fill], axis=0)
+
+
+def pin(*arrays):
+    return [pltpu.with_memory_space_constraint(a, pltpu.HBM) for a in arrays]
 
 
 def local(R, C, x, u, gain, proj, taps, sharp, final):
@@ -563,7 +567,7 @@
         compiler_params=pltpu.CompilerParams(
             collective_id=0, has_side_effects=True, vmem_limit_bytes=56203673
         ),
-    )(x, u, gain, proj, taps, sharp, final)
+    )(*pin(x, u, gain, proj, taps), sharp, *pin(final))
     return (out, gain_sum.reshape(ch), taps_sum.reshape(3, 3, c3), sharp_sum[0, :heads])
 
 

time: 49.3 us -> 47.8 us (0.970)
  local copies, waits for them, and re-layouts: 3.91 us -> 2.48 us
    unnamed x7 -> x3, local copies, waits for them, and re-layouts: 2.75 us -> 1.32 us
where the time goes in v3:
time: 47.8 us; the launch traced here: 47.6 us
  Pallas kernels  43.9 us (92%)
  local copies, waits for them, and re-layouts  2.48 us (5%)
  between operations  0.65 us (1%)
  other arithmetic  0.6 us (1%)
    pallas_call x1, Pallas kernels, local(): pl.pallas_call(functools.partial(kernel, (R, C, H, B, ch, heads)), name='...  43.9 us
    unnamed x3, local copies, waits for them, and re-layouts  1.32 us

profile of v3, /device:TPU:0, one launch (start us, length us, event | category | flops | bytes accessed | tf_op | source)
XLA Modules:
  0.0 47.6 jit_solution(2117210546195407750)
XLA Ops:
  0.6 0.0 copy-start
  0.6 0.6 %copy-done = f32[8]{0:T(128)S(1)} copy-done((f32[8]{0:T(128)S(1)}, f32[8]{0:T(128)}, u32[]{:S(2)}) %copy-start) | copy-done | bytes 56
  1.3 43.9 %attention_backward.1 = (bf16[8,32,384]{2,1,0:T(8,128)(2,1)S(1)}, f32[1,384]{1,0:T(1,128)S(1)}, f32[9,1152]{1,0:T(8,128)S(1)}, f32[1,128]{1,0:T(1,128)S(1)}) custom-call(bf16[8,32,384]{2,1,0:T(8,128)(2,1)} %x_hbm.1, bf16[8,32,384]{2,1,0:T(8,128)(2,1)} %u_hbm.1, f32[384]{0:T(512)} %gain_hbm.1, bf16[384,1152]{1,0:T(8,128)(2,1)} %proj_hbm.1, ...), custom_call_target="tpu_custom_call" | custom-call | tf_op jit(solution)/shard_map/attention_backward/pallas_call | solution.py:515
  45.2 0.5 %slice_bitcast_fusion = f32[8]{0:T(128)} fusion(f32[1,128]{1,0:T(1,128)S(1)} %get-tuple-element.11), kind=kLoop, calls=%fused_computation | loop fusion | bytes 64 | tf_op jit(solution)/shard_map/squeeze | solution.py:571
  45.7 0.6 %reduce = f32[384]{0:T(512)} reduce(f32[1,384]{1,0:T(1,128)S(1)} %get-tuple-element.9, f32[]{:T(128)} %constant), dimensions={0}, to_apply=%get-tuple-element.9.reduce_sub_computation | reduce | bytes 3076 | tf_op jit(solution)/shard_map/attention_backward/pallas_call | solution.py:515
  46.3 0.6 %reshape.15 = f32[3,3,1152]{2,1,0:T(4,128)} reshape(f32[9,1152]{1,0:T(8,128)S(1)} %get-tuple-element.10) | data formatting | bytes 82944 | tf_op jit(solution)/shard_map/reshape | solution.py:571
  46.9 0.7 %copy.12 = bf16[8,32,384]{2,1,0:T(8,128)(2,1)} copy(bf16[8,32,384]{2,1,0:T(8,128)(2,1)S(1)} %get-tuple-element.16) | data formatting | bytes 393216
Async XLA Ops:
  0.6 0.7 %copy-start = (f32[8]{0:T(128)S(1)}, f32[8]{0:T(128)}, u32[]{:S(2)}) copy-start(f32[8]{0:T(128)} %sharp_ref.1) | copy-start | bytes 100
